TPU v7x, 32 devices: a whole 2x2x4 slice. The times are simulated.
32 devices in a mesh: grid: 2 (over core), pts: 16 (over z, y, x).
Axes of the slice: x: 2, y: 2, z: 4, core: 2. Of those that a mesh axis runs over, the one named last changes fastest.
Arguments:
- spectrum: float32 [2, 7168, 1152], P('grid', 'pts'), may hold values from 0.1 to 1
- interaction: bfloat16 [1152, 1152], replicated, may hold values from -0.1875 to 0.1875
- comp_speed: float32 [2, 1152], replicated, may hold values from -0.45 to 0.45
- sea_mask: int32 [2, 7168], replicated, may hold values 0 or 1
- stokes_kernel: float32 [1152, 80], replicated, may hold values from -0.1875 to 0.1875
- tile_owner: int32 [2, 7168, 1], P('grid', 'pts'), may hold values from 0 to 15; in each aligned block of 448 rows (0 to 447, 448 to 895, ..., all dimensions but the last counted through in order) at most 56 rows name the same one
- ocean_column: int32 [2, 7168], P('grid', 'pts'), may hold values from 0 to 255
- neighbours: int32 [2, 4096, 4], P('grid', 'pts'), may hold values from 0 to 255
- coriolis: float32 [2, 4096], P('grid', 'pts'), may hold values from -1 to 1
- velocity: float32 [2, 2, 40, 4096], P('grid', None, None, 'pts'), may hold values from -6 to 6
Outputs:
- spectrum_next: float32 [2, 7168, 1152], P('grid', 'pts')
- velocity_next: float32 [2, 2, 40, 4096], P('grid', None, None, 'pts')
Inputs may be any that keep to these rules, and one draw needn't show every extreme that they name: `tile_owner`: at most 56 of the rows of one device name the same tile, and some tile takes exactly 56 of them.
All inputs are finite; a program needn't handle non-finite values.
Results may differ from a plain program's by a relative error of at most 0.0003.
Values sent between devices are 32-bit elements; how exact they have to be, the bound alone decides.
No kernel may reach another device: no remote copies, remote signals or barrier semaphores. Data moves between devices by JAX's collectives and lax.ppermute only.
A program may use at most 128 MiB of HBM per device.

v0:
```python
import jax
import jax.numpy as jnp
from jax import lax
from jax.sharding import PartitionSpec as P

GC = 256
SUBSTEPS = 4


def from_partner(value, axis, bit):
    mask = 2**bit
    pairs = [(source, source ^ mask) for source in range(lax.axis_size(axis))]
    return lax.ppermute(value, axis, pairs)


def shift_outer(field, amount):
    length = field.shape[2]
    if amount == 0:
        return field
    if amount > 0:
        padded = jnp.pad(field, ((0, 0), (0, 0), (amount, 0)))
        return padded[:, :, :length]
    padded = jnp.pad(field, ((0, 0), (0, 0), (0, -amount)))
    return padded[:, :, -amount:]


def flat_shift(field, amount):
    inner = field.shape[1]
    outer_step = amount // inner
    remain = amount % inner
    moved = shift_outer(field, outer_step)
    if remain == 0:
        return moved
    carried = shift_outer(field, outer_step + 1)
    return jnp.concatenate([carried[:, inner - remain :], moved[:, : inner - remain]], axis=1)


def advect(field, speed_x, speed_y, mask, not_first, not_last, upper, lower):
    left = flat_shift(field, 1) * not_first
    right = flat_shift(field, -1) * not_last
    sx = speed_x[:, None, None]
    sy = speed_y[:, None, None]
    result = field - jnp.maximum(sx, 0.0) * (field - upper) - jnp.minimum(sx, 0.0) * (lower - field)
    result = result - jnp.maximum(sy, 0.0) * (field - left) - jnp.minimum(sy, 0.0) * (right - field)
    return result * mask


def column_masks(inner, outer):
    flat_index = (
        jnp.arange(outer, dtype=jnp.int32)[None, :] * inner
        + jnp.arange(inner, dtype=jnp.int32)[:, None]
    )
    column = flat_index % GC
    return ((column != 0).astype(jnp.float32), (column != GC - 1).astype(jnp.float32))


def select_columns(flow, chosen):
    columns = flow.shape[1]
    picker = (jnp.arange(columns, dtype=jnp.int32)[:, None] == chosen[None, :]).astype(jnp.float32)
    return jnp.dot(
        flow, picker, precision=lax.Precision.HIGHEST, preferred_element_type=jnp.float32
    )


def per_device(
    spectrum,
    interaction,
    comp_speed,
    sea_mask,
    stokes_kernel,
    tile_owner,
    ocean_column,
    neighbours,
    coriolis,
    velocity,
):
    local = spectrum[0]
    held = local.shape[0]
    comps = local.shape[1]
    mix = jnp.dot(local.astype(jnp.bfloat16), interaction, preferred_element_type=jnp.float32)
    relaxed = local + 0.5 * local * jnp.tanh(mix)
    transposed = relaxed.T
    grid_index = lax.axis_index("grid")
    width = lax.axis_size("pts")
    share = comps // width
    sent = transposed.reshape(width, share, held)
    field = lax.all_to_all(sent, "pts", split_axis=0, concat_axis=2, tiled=True)[0].reshape(
        share, width, held
    )
    grid_mask = lax.dynamic_index_in_dim(sea_mask, grid_index, 0, keepdims=False)
    mask = grid_mask.reshape(held, width).T.astype(jnp.float32)[None]
    not_first, not_last = column_masks(width, held)
    speeds = lax.dynamic_slice_in_dim(comp_speed, lax.axis_index("pts") * share, share, 1)
    depth = -(-GC // width)
    for step in range(SUBSTEPS):
        slabs = jnp.stack([field[:, :, :depth], field[:, :, held - depth :]], axis=1)
        other = from_partner(slabs, "grid", 0)
        empty = jnp.zeros_like(other[:, 0])
        top_slab = jnp.where(grid_index == 1, other[:, 1], empty)
        bottom_slab = jnp.where(grid_index == 0, other[:, 0], empty)
        upper = flat_shift(jnp.concatenate([top_slab, field], axis=2), GC)[:, :, depth:]
        lower = flat_shift(jnp.concatenate([field, bottom_slab], axis=2), -GC)[:, :, :held]
        field = advect(
            field, speeds[0], speeds[1], mask, not_first[None], not_last[None], upper, lower
        )
    dealt = field.reshape(share, width * held)
    returned = lax.all_to_all(dealt[None], "pts", split_axis=2, concat_axis=0, tiled=True)
    spectrum_next = returned.reshape(comps, held).T
    stokes = jnp.dot(
        spectrum_next,
        stokes_kernel,
        precision=lax.Precision.HIGHEST,
        preferred_element_type=jnp.float32,
    )
    tiles = lax.axis_size("pts")
    capacity = 2 * held // tiles
    owner = tile_owner[0, :, 0]
    position = jnp.arange(held, dtype=jnp.int32)
    earlier = (owner[:, None] == owner[None, :]) & (position[None, :] < position[:, None])
    rank = jnp.sum(earlier.astype(jnp.int32), axis=1)
    slot = owner * capacity + rank
    placer = (slot[:, None] == jnp.arange(tiles * capacity, dtype=jnp.int32)[None, :]).astype(
        jnp.float32
    )
    payload = jnp.concatenate([stokes, (ocean_column[0] + 1)[:, None].astype(jnp.float32)], axis=1)
    buffer = jnp.dot(
        placer.T, payload, precision=lax.Precision.HIGHEST, preferred_element_type=jnp.float32
    )
    buffer = buffer.reshape(tiles, capacity, payload.shape[1])
    received = lax.all_to_all(buffer, "pts", split_axis=0, concat_axis=0, tiled=True).reshape(
        tiles * capacity, payload.shape[1]
    )
    columns = coriolis.shape[1]
    target = received[:, -1].astype(jnp.int32) - 1
    onehot = (jnp.arange(columns, dtype=jnp.int32)[:, None] == target[None, :]).astype(jnp.float32)
    drift_sum = jnp.dot(
        onehot,
        received[:, :-1],
        precision=lax.Precision.HIGHEST,
        preferred_element_type=jnp.float32,
    )
    count = jnp.sum(onehot, axis=1)
    drift = (drift_sum / jnp.maximum(count, 1.0)[:, None]).T
    levels = drift.shape[0] // 2
    east_drift = drift[:levels]
    north_drift = drift[levels:]
    near = neighbours[0]
    east_flow = velocity[0, 0]
    north_flow = velocity[0, 1]
    zeta = (
        select_columns(north_flow, near[:, 0])
        - select_columns(north_flow, near[:, 1])
        - (select_columns(east_flow, near[:, 2]) - select_columns(east_flow, near[:, 3]))
    )
    spin = coriolis[0][None, :]
    new_east = east_flow + 0.25 * (spin * north_flow + (spin + zeta) * north_drift)
    new_north = north_flow - 0.25 * (spin * east_flow + (spin + zeta) * east_drift)
    return (spectrum_next[None], jnp.stack([new_east, new_north])[None])


def solution(mesh):
    placed = (
        P("grid", "pts", None),
        P(),
        P(),
        P(),
        P(),
        P("grid", "pts", None),
        P("grid", "pts"),
        P("grid", "pts", None),
        P("grid", "pts"),
        P("grid", None, None, "pts"),
    )
    return jax.shard_map(
        per_device,
        mesh=mesh,
        in_specs=placed,
        out_specs=(P("grid", "pts", None), P("grid", None, None, "pts")),
        check_vma=False,
    )
```

profile of v0, /device:TPU:0, one launch (start us, length us, event | category | flops | bytes accessed | tf_op | source)
XLA Modules:
  0.0 254.2 jit_solution(3096730168442478846)
XLA Ops:
  0.6 1.7 copy-done
  2.4 5.1 %fusion.2 = f32[1152,448]{0,1:T(8,128)} fusion(bf16[1152,1152]{1,0:T(8,128)(2,1)S(1)} %copy-done, f32[1,448,1152]{2,1,0:T(8,128)} %param.10), kind=kOutput, calls=%fused_computation.3 | convolution fusion | flops 1191149568 | bytes 6782976 | tf_op jit(solution)/shard_map/dot_general | solution.py:80
  7.5 3.1 %copy.49 = f32[1152,448]{1,0:T(8,128)} copy(f32[1152,448]{0,1:T(8,128)} %fusion.2) | data formatting | bytes 4128768 | tf_op jit(solution)/shard_map/transpose | solution.py:82
  10.6 8.5 %all-to-all-start = ((f32[16,72,448]{2,1,0:T(8,128)}), f32[16,72,448]{2,1,0:T(8,128)S(1)}, u32[]{:S(2)}, u32[]{:S(2)}) async-start(f32[16,72,448]{2,1,0:T(8,128)} %bitcast.115), calls=%async_computation | async-start | bytes 4718592 | tf_op jit(solution)/shard_map/all_to_all | solution.py:87
  19.5 0.8 constant_dynamic-slice_fusion
  20.3 46.4 %all-to-all-done = f32[16,72,448]{2,1,0:T(8,128)S(1)} async-done(((f32[16,72,448]{2,1,0:T(8,128)}), f32[16,72,448]{2,1,0:T(8,128)S(1)}, u32[]{:S(2)}, u32[]{:S(2)}) %all-to-all-start) | async-done | bytes 2064416 | tf_op jit(solution)/shard_map/all_to_all | solution.py:87
  66.7 1.0 slice_bitcast_fusion.7
  67.7 1.2 copy.50
  68.9 0.2 copy.51
  69.3 2.7 %fusion.100 = (f32[72,15,448]{2,0,1:T(8,128)}, f32[72,15,448]{2,0,1:T(8,128)}) fusion(f32[72,16,448]{2,0,1:T(8,128)S(1)} %bitcast.109), kind=kLoop, calls=%fused_computation.179 | loop fusion | bytes 7741440 | tf_op jit(solution)/shard_map/slice | solution.py:35
  72.0 0.1 pad_slice_fusion.6
  72.1 0.7 fusion.104
  72.8 1.1 copy.77
  73.9 1.0 copy.78
  75.0 1.3 select_bitcast_fusion.6
  76.3 0.5 copy-done.7
  76.8 3.9 %fusion.35 = f32[72,16,448]{2,0,1:T(8,128)S(1)} fusion(f32[72,16,448]{2,0,1:T(8,128)S(1)} %bitcast.111, f32[72,16,16]{2,0,1:T(8,128)S(1)} %get-tuple-element.54, f32[72,16,16]{2,0,1:T(8,128)S(1)} %get-tuple-element.55, f32[72,15,448]{2,0,1:T(8,128)} %get-tuple-element.29, f32[72,1,448]{2,0,1:T(8,128)S(1)} %get-tuple-element.31, ...), kind=kLoop, calls=%fused_computation.43 | loop fusion | flops 9805824 | bytes 8492160 | tf_op jit(solution)/shard_map/mul | solution.py:45
  80.7 1.4 copy-done.2
  82.1 0.2 slice_bitcast_fusion.5
  82.3 0.2 copy.55
  82.5 0.2 copy.56
  82.8 0.4 collective-permute-start.1
  83.1 5.0 %fusion.99 = (f32[72,15,448]{2,0,1:T(8,128)}, f32[72,15,448]{2,0,1:T(8,128)}) fusion(f32[72,16,448]{2,0,1:T(8,128)} %copy-done.2), kind=kLoop, calls=%fused_computation.178 | loop fusion | bytes 7741440 | tf_op jit(solution)/shard_map/slice | solution.py:35
  88.4 1.0 copy.79
  89.5 1.0 copy.80
  90.5 1.1 select_bitcast_fusion.4
  91.6 4.3 %fusion.26 = f32[72,16,448]{2,0,1:T(8,128)S(1)} fusion(f32[72,16,448]{2,0,1:T(8,128)S(1)} %copy-done.3, f32[72,16,16]{2,0,1:T(8,128)S(1)} %select_bitcast_fusion.4, f32[72,16,16]{2,0,1:T(8,128)S(1)} %select_bitcast_fusion.5, f32[72,15,448]{2,0,1:T(8,128)} %get-tuple-element.23, f32[72,1,448]{2,0,1:T(8,128)S(1)} %get-tuple-element.25, ...), kind=kLoop, calls=%fused_computation.32 | loop fusion | flops 9805824 | bytes 8492160 | tf_op jit(solution)/shard_map/mul | solution.py:45
  95.9 1.4 copy-done.4
  97.3 0.2 slice_bitcast_fusion.3
  97.5 0.2 copy.59
  97.7 0.2 copy.60
  98.0 0.2 collective-permute-start.2
  98.2 5.0 %fusion.98 = (f32[72,15,448]{2,0,1:T(8,128)}, f32[72,15,448]{2,0,1:T(8,128)}) fusion(f32[72,16,448]{2,0,1:T(8,128)} %copy-done.4), kind=kLoop, calls=%fused_computation.177 | loop fusion | bytes 7741440 | tf_op jit(solution)/shard_map/slice | solution.py:35
  103.4 0.2 copy.81
  103.6 0.2 copy.82
  103.9 6.0 %fusion.17 = f32[72,16,448]{2,0,1:T(8,128)S(1)} fusion(f32[72,16,448]{2,0,1:T(8,128)} %copy-done.4, f32[72,16,16]{2,0,1:T(8,128)S(1)} %select_bitcast_fusion.2, f32[72,16,16]{2,0,1:T(8,128)S(1)} %select_bitcast_fusion.3, f32[72,15,448]{2,0,1:T(8,128)} %get-tuple-element.17, f32[72,1,448]{2,0,1:T(8,128)S(1)} %get-tuple-element.19, ...), kind=kLoop, calls=%fused_computation.21 | loop fusion | flops 9805824 | bytes 8492160 | tf_op jit(solution)/shard_map/mul | solution.py:45
  109.9 1.0 slice_bitcast_fusion.1
  110.9 1.2 copy.63
  112.1 0.2 copy.64
  112.4 0.5 collective-permute-start.3
  112.9 2.7 %fusion.97 = (f32[72,15,448]{2,0,1:T(8,128)}, f32[72,15,448]{2,0,1:T(8,128)}) fusion(f32[72,16,448]{2,0,1:T(8,128)S(1)} %fusion.17), kind=kLoop, calls=%fused_computation.176 | loop fusion | bytes 7741440 | tf_op jit(solution)/shard_map/slice | solution.py:35
  115.8 1.0 copy.83
  116.9 1.0 copy.84
  118.0 1.1 select_bitcast_fusion
  119.1 5.3 %fusion.8 = f32[72,16,448]{2,0,1:T(8,128)} fusion(f32[72,16,448]{2,0,1:T(8,128)S(1)} %fusion.17, f32[72,16,16]{2,0,1:T(8,128)S(1)} %select_bitcast_fusion, f32[72,16,16]{2,0,1:T(8,128)S(1)} %select_bitcast_fusion.1, f32[72,15,448]{2,0,1:T(8,128)} %get-tuple-element.11, f32[72,1,448]{2,0,1:T(8,128)S(1)} %get-tuple-element.13, ...), kind=kLoop, calls=%fused_computation.10 | loop fusion | flops 9805824 | bytes 8492160 | tf_op jit(solution)/shard_map/mul | solution.py:45
  124.4 3.6 %copy.74 = f32[72,16,448]{0,2,1:T(8,128)} copy(f32[72,16,448]{2,0,1:T(8,128)} %fusion.8) | data formatting | bytes 4128768 | tf_op jit(solution)/shard_map/broadcast_in_dim;reshape | solution.py:107
  128.0 11.3 %all-to-all-start.1 = ((f32[1,72,7168]{1,0,2:T(1,128)}), f32[1,72,7168]{1,0,2:T(1,128)}, u32[]{:S(2)}, u32[]{:S(2)}) async-start(f32[1,72,7168]{1,0,2:T(1,128)} %bitcast.114), calls=%async_computation.1 | async-start | bytes 7340032 | tf_op jit(solution)/shard_map/all_to_all | solution.py:107
  139.4 0.2 convert_reduce_fusion.1
  139.7 70.2 %all-to-all-done.1 = f32[1,72,7168]{1,0,2:T(1,128)} async-done(((f32[1,72,7168]{1,0,2:T(1,128)}), f32[1,72,7168]{1,0,2:T(1,128)}, u32[]{:S(2)}, u32[]{:S(2)}) %all-to-all-start.1) | async-done | bytes 2064416 | tf_op jit(solution)/shard_map/all_to_all | solution.py:107
  209.9 4.3 %copy.75 = f32[1,72,16,448]{3,2,1,0:T(8,128)} copy(f32[1,72,16,448]{1,3,2,0:T(8,128)} %bitcast.30) | data formatting | bytes 4128768 | tf_op jit(solution)/shard_map/all_to_all | solution.py:107
  214.2 3.1 %copy.70 = f32[16,1,72,448]{3,2,0,1:T(8,128)S(1)} copy(f32[16,1,72,448]{3,0,2,1:T(8,128)} %bitcast.116) | data formatting | bytes 4128768 | tf_op jit(solution)/shard_map/all_to_all | solution.py:107
  217.3 1.7 fusion.108
  219.0 2.0 fusion.60
  221.0 18.0 %all-to-all-start.2 = ((f32[16,56,81]{2,1,0:T(8,128)}), f32[16,56,81]{2,1,0:T(8,128)S(1)}, u32[]{:S(2)}, u32[]{:S(2)}) async-start(f32[16,56,81]{2,1,0:T(8,128)} %bitcast.120), calls=%async_computation.2 | async-start | bytes 917504 | tf_op jit(solution)/shard_map/all_to_all | solution.py:130
  239.0 0.2 fusion.67
  239.2 0.2 fusion.68
  239.5 0.2 convolution_subtract_fusion.1
  239.7 3.1 %copy.72 = f32[1,448,1152]{2,1,0:T(8,128)} copy(f32[1,448,1152]{1,2,0:T(8,128)} %bitcast.113) | data formatting | bytes 4128768
  242.8 9.4 %all-to-all-done.2 = f32[16,56,81]{2,1,0:T(8,128)S(1)} async-done(((f32[16,56,81]{2,1,0:T(8,128)}), f32[16,56,81]{2,1,0:T(8,128)S(1)}, u32[]{:S(2)}, u32[]{:S(2)}) %all-to-all-start.2) | async-done | bytes 290336 | tf_op jit(solution)/shard_map/all_to_all | solution.py:130
  252.2 0.3 fusion.64
  252.5 0.2 convert_reduce_fusion
  252.7 0.6 convolution_divide_fusion
  253.3 0.2 fusion.83
  253.5 0.6 maximum_bitcast_fusion
  (55 shorter events, 1.3 us)
Async XLA Ops:
  0.6 1.8 copy-start
  10.6 8.5 %copy-start.11 = (s32[2,7168]{1,0:T(2,128)S(1)}, s32[2,7168]{1,0:T(2,128)}, u32[]{:S(2)}) copy-start(s32[2,7168]{1,0:T(2,128)} %param.13) | copy-start | bytes 172036
  10.6 56.0 %all-to-all-start = ((f32[16,72,448]{2,1,0:T(8,128)}), f32[16,72,448]{2,1,0:T(8,128)S(1)}, u32[]{:S(2)}, u32[]{:S(2)}) async-start(f32[16,72,448]{2,1,0:T(8,128)} %bitcast.115), calls=%async_computation | async-start | bytes 4718592 | tf_op jit(solution)/shard_map/all_to_all | solution.py:87
  69.2 2.9 %collective-permute-start = (f32[72,2,16,16]{0,3,2,1:T(8,128)S(1)}, f32[72,2,16,16]{0,3,2,1:T(8,128)S(1)}, u32[]{:S(2)}, u32[]{:S(2)}) collective-permute-start(f32[72,2,16,16]{0,3,2,1:T(8,128)S(1)} %pad_maximum_fusion.8), channel_id=1, source_target_pairs={{0,16},{16,0},{1,17},{17,1},{2,18},{18,2},{3,19},{19,3},{4,20},{20... | collective-permute-start | bytes 442376 | tf_op jit(solution)/shard_map/ppermute | solution.py:13
  75.0 1.8 copy-start.7
  80.7 1.4 copy-start.2
  82.8 5.4 %copy-start.3 = (f32[72,16,448]{2,0,1:T(8,128)S(1)}, f32[72,16,448]{2,0,1:T(8,128)}, u32[]{:S(2)}) copy-start(f32[72,16,448]{2,0,1:T(8,128)} %copy-done.2) | copy-start | bytes 6193156
  82.8 5.6 %collective-permute-start.1 = (f32[72,2,16,16]{0,3,2,1:T(8,128)S(1)}, f32[72,2,16,16]{0,3,2,1:T(8,128)S(1)}, u32[]{:S(2)}, u32[]{:S(2)}) collective-permute-start(f32[72,2,16,16]{0,3,2,1:T(8,128)S(1)} %pad_maximum_fusion.9), channel_id=1, source_target_pairs={{0,16},{16,0},{1,17},{17,1},{2,18},{18,2},{3,19},{19,3},{4,20},{20... | collective-permute-start | bytes 442376 | tf_op jit(solution)/shard_map/ppermute | solution.py:13
  95.9 1.4 copy-start.4
  98.0 5.2 %copy-start.5 = (f32[72,16,448]{2,0,1:T(8,128)S(1)}, f32[72,16,448]{2,0,1:T(8,128)}, u32[]{:S(2)}) copy-start(f32[72,16,448]{2,0,1:T(8,128)} %copy-done.4) | copy-start | bytes 6193156
  98.0 5.3 %collective-permute-start.2 = (f32[72,2,16,16]{0,3,2,1:T(8,128)S(1)}, f32[72,2,16,16]{0,3,2,1:T(8,128)S(1)}, u32[]{:S(2)}, u32[]{:S(2)}) collective-permute-start(f32[72,2,16,16]{0,3,2,1:T(8,128)S(1)} %pad_maximum_fusion.10), channel_id=1, source_target_pairs={{0,16},{16,0},{1,17},{17,1},{2,18},{18,2},{3,19},{19,3},{4,20},{20... | collective-permute-start | bytes 442376 | tf_op jit(solution)/shard_map/ppermute | solution.py:13
  112.4 3.4 %collective-permute-start.3 = (f32[72,2,16,16]{0,3,2,1:T(8,128)S(1)}, f32[72,2,16,16]{0,3,2,1:T(8,128)S(1)}, u32[]{:S(2)}, u32[]{:S(2)}) collective-permute-start(f32[72,2,16,16]{0,3,2,1:T(8,128)S(1)} %pad_maximum_fusion.11), channel_id=1, source_target_pairs={{0,16},{16,0},{1,17},{17,1},{2,18},{18,2},{3,19},{19,3},{4,20},{20... | collective-permute-start | bytes 442376 | tf_op jit(solution)/shard_map/ppermute | solution.py:13
  128.0 11.3 %copy-start.10 = (s32[1,448,1]{1,2,0:T(1,128)S(1)}, s32[1,448,1]{1,2,0:T(1,128)}, u32[]{:S(2)}) copy-start(s32[1,448,1]{1,2,0:T(1,128)} %param.15) | copy-start | bytes 5380
  128.0 11.6 %copy-start.14 = (s32[1,448]{1,0:T(1,128)S(1)}, s32[1,448]{1,0:T(1,128)}, u32[]{:S(2)}) copy-start(s32[1,448]{1,0:T(1,128)} %param.16) | copy-start | bytes 5380
  128.0 11.6 %copy-start.13 = (s32[1,256,4]{1,2,0:T(4,128)S(1)}, s32[1,256,4]{1,2,0:T(4,128)}, u32[]{:S(2)}) copy-start(s32[1,256,4]{1,2,0:T(4,128)} %param.17) | copy-start | bytes 12292
  128.0 81.8 %all-to-all-start.1 = ((f32[1,72,7168]{1,0,2:T(1,128)}), f32[1,72,7168]{1,0,2:T(1,128)}, u32[]{:S(2)}, u32[]{:S(2)}) async-start(f32[1,72,7168]{1,0,2:T(1,128)} %bitcast.114), calls=%async_computation.1 | async-start | bytes 7340032 | tf_op jit(solution)/shard_map/all_to_all | solution.py:107
  214.2 3.1 %copy-start.8 = (f32[1152,80]{0,1:T(8,128)S(1)}, f32[1152,80]{0,1:T(8,128)}, u32[]{:S(2)}) copy-start(f32[1152,80]{0,1:T(8,128)} %param.14) | copy-start | bytes 1105924
  217.3 21.9 %copy-start.6 = (f32[16,1,72,448]{3,2,0,1:T(8,128)}, f32[16,1,72,448]{3,2,0,1:T(8,128)S(1)}, u32[]{:S(2)}) copy-start(f32[16,1,72,448]{3,2,0,1:T(8,128)S(1)} %copy.70) | copy-start | bytes 6193156
  217.3 21.7 %copy-start.9 = (f32[1,2,40,256]{3,2,1,0:T(8,128)S(1)}, f32[1,2,40,256]{3,2,1,0:T(8,128)}, u32[]{:S(2)}) copy-start(f32[1,2,40,256]{3,2,1,0:T(8,128)} %param.19) | copy-start | bytes 245764
  221.0 31.2 %all-to-all-start.2 = ((f32[16,56,81]{2,1,0:T(8,128)}), f32[16,56,81]{2,1,0:T(8,128)S(1)}, u32[]{:S(2)}, u32[]{:S(2)}) async-start(f32[16,56,81]{2,1,0:T(8,128)} %bitcast.120), calls=%async_computation.2 | async-start | bytes 917504 | tf_op jit(solution)/shard_map/all_to_all | solution.py:130
  239.7 14.5 %copy-start.1 = (bf16[1152,1152]{1,0:T(8,128)(2,1)S(1)}, bf16[1152,1152]{1,0:T(8,128)(2,1)}, u32[]{:S(2)}) copy-start(bf16[1152,1152]{1,0:T(8,128)(2,1)} %param.11) | copy-start | bytes 7962628
  239.7 13.6 %copy-start.12 = (f32[1,256]{1,0:T(1,128)S(1)}, f32[1,256]{1,0:T(1,128)}, u32[]{:S(2)}) copy-start(f32[1,256]{1,0:T(1,128)} %param.18) | copy-start | bytes 3076
where the time goes:
time: 255 us; the launch traced here: 254 us
  waiting for transfers between devices  126 us (49%)
  local copies, waits for them, and re-layouts  53.1 us (21%)
  starting transfers between devices  39 us (15%)
  other arithmetic  24.8 us (10%)
  matrix products  10.2 us (4%)
    all_to_all x1, waiting for transfers between devices, per_device(): lax.all_to_all(dealt[None], 'pts', split_axis=2, concat_axis=0, tiled=True)  70.2 us
    all_to_all x1, waiting for transfers between devices, per_device(): lax.all_to_all(sent, 'pts', split_axis=0, concat_axis=2, tiled=True)[0]  46.4 us
    mul x4, other arithmetic, advect(): return result * mask  19.4 us
    all_to_all x1, starting transfers between devices, per_device(): lax.all_to_all(buffer, 'pts', split_axis=0, concat_axis=0, tiled=True)  18 us
    slice x4, local copies, waits for them, and re-layouts, flat_shift(): carried[:, inner - remain:]  15.4 us
    unnamed x39, local copies, waits for them, and re-layouts  15 us
    all_to_all x1, starting transfers between devices, per_device(): lax.all_to_all(dealt[None], 'pts', split_axis=2, concat_axis=0, tiled=True)  11.3 us
    all_to_all x1, waiting for transfers between devices, per_device(): lax.all_to_all(buffer, 'pts', split_axis=0, concat_axis=0, tiled=True)  9.38 us
  transfers between devices with their start and end apart: 7, of which 3 were waited for; matrix products, arithmetic and copies ran while one was open for 8% of the time, Pallas kernels for 0%

commit v1 on v0

v1 whole, which is shorter than its diff:
```python
import functools

import jax
import jax.numpy as jnp
from jax import lax
from jax.experimental import pallas as pl
from jax.experimental.pallas import tpu as pltpu
from jax.sharding import PartitionSpec as P


GC = 256
SUBSTEPS = 4
LANES = 128
SUBLANES = 8
SPLIT = (5, 4)
F32 = jnp.float32
BF16 = jnp.bfloat16

VMEM = pltpu.MemorySpace.VMEM
SMEM = pltpu.MemorySpace.SMEM


def round_up(value, unit):
    return -(-value // unit) * unit


def params():
    return pltpu.CompilerParams(vmem_limit_bytes=48 * 1024 * 1024)


def whole_vmem(count):
    return [pl.BlockSpec(memory_space=VMEM)] * count


def split_units(units):
    total = sum(SPLIT)
    edges = [0]
    for end in range(1, len(SPLIT) + 1):
        edges.append(max(edges[-1], round(sum(SPLIT[:end]) * units / total)))
    return [b - a for a, b in zip(edges[:-1], edges[1:]) if b > a]


def halves(value):
    high = value.astype(BF16)
    low = (value - high.astype(F32)).astype(BF16)
    return high, low


def unit_of(group):
    return 2 * SUBLANES * group


def relax_kernel(group, held, offset, spectrum, weights, out, rounded, turned):
    width = weights.shape[1]
    unit = unit_of(group)
    rounded[...] = spectrum[...].astype(BF16)
    for start in range(0, width, 256):
        size = min(256, width - start)
        mix = jnp.dot(
            rounded[...], weights[:, start : start + size], preferred_element_type=F32
        )
        local = spectrum[:, offset + start : offset + start + size]
        relaxed = local + 0.5 * local * jnp.tanh(mix)
        turned[start : start + size, :] = relaxed.T
    for start in range(0, width, unit):
        row = start // unit * SUBLANES
        for part in range(group):
            base = start + part * 2 * SUBLANES
            out[part, row : row + SUBLANES, :held] = turned[base : base + SUBLANES, :]
            out[part, row : row + SUBLANES, held:] = turned[
                base + SUBLANES : base + 2 * SUBLANES, :
            ]


def relax(spectrum, weights, group, first, units):
    held, comps = spectrum.shape
    unit = unit_of(group)
    offset, width = first * unit, units * unit
    block = (group, units * SUBLANES, 2 * held)
    return pl.pallas_call(
        functools.partial(relax_kernel, group, held, offset),
        grid=(1,),
        out_shape=jax.ShapeDtypeStruct(block, F32),
        in_specs=[
            pl.BlockSpec((held, comps), lambda i: (0, 0)),
            pl.BlockSpec((pl.Element(comps), pl.Element(width)), lambda i: (0, offset)),
        ],
        out_specs=pl.BlockSpec(block, lambda i: (0, 0, 0)),
        scratch_shapes=[pltpu.VMEM((held, comps), BF16), pltpu.VMEM((width, held), F32)],
        compiler_params=params(),
        name="relax",
    )(spectrum, weights)


def edge_rows(source, target, held, tall, first):
    base = 0 if first else held - tall
    for col in range(source.shape[0]):
        target[col, :, :tall] = source[col, :, base : base + tall]
        target[col, :, tall : 2 * tall] = source[col, :, held + base : held + base + tall]


def edge_kernel(held, tall, place, source, edge):
    rest = edge.shape[2] - 2 * tall
    if rest:
        edge[:, :, 2 * tall :] = jnp.zeros((edge.shape[0], edge.shape[1], rest), F32)

    @pl.when(place[1] == 0)
    def _():
        edge_rows(source, edge, held, tall, False)

    @pl.when(place[1] == 1)
    def _():
        edge_rows(source, edge, held, tall, True)


def edges_of(place, source, tall, edge_lanes):
    count, rows, width = source.shape
    return pl.pallas_call(
        functools.partial(edge_kernel, width // 2, tall),
        out_shape=jax.ShapeDtypeStruct((count, rows, edge_lanes), F32),
        in_specs=[pl.BlockSpec(memory_space=SMEM)] + whole_vmem(1),
        out_specs=pl.BlockSpec(memory_space=VMEM),
        compiler_params=params(),
        name="edge",
    )(place, source)


def pick_kernel(group, held, step, place, own, speeds, send):
    width = own.shape[2]
    lane = lax.broadcasted_iota(jnp.int32, (SUBLANES, width), 1)
    tiles = width // LANES

    def spread(part):
        return jnp.concatenate([speeds[0, part, 1]] * tiles, axis=1)

    forward = jnp.where(lane < held, spread(0), spread(1)) > 0.0
    spot = lax.rem(lane, step)

    @pl.when(place[0] == 1)
    def _():
        for col in range(SUBSTEPS):
            last = pltpu.roll(own[group - SUBSTEPS + col], 1, 1)
            last = jnp.where(spot == 0, 0.0, last)
            send[col] = jnp.where(forward, last, own[col])

    @pl.when(place[0] == 0)
    def _():
        for col in range(SUBSTEPS):
            first = pltpu.roll(own[col], width - 1, 1)
            first = jnp.where(spot == step - 1, 0.0, first)
            send[col] = jnp.where(forward, own[group - SUBSTEPS + col], first)


def pick(place, own, speeds, first, units, step):
    group, _, width = own.shape
    return pl.pallas_call(
        functools.partial(pick_kernel, group, width // 2, step),
        grid=(units,),
        out_shape=jax.ShapeDtypeStruct((SUBSTEPS, units * SUBLANES, width), F32),
        in_specs=[
            pl.BlockSpec(memory_space=SMEM),
            pl.BlockSpec((group, SUBLANES, width), lambda i: (0, i, 0)),
            pl.BlockSpec((1, 2, 2, SUBLANES, LANES), lambda i: (i + first, 0, 0, 0, 0)),
        ],
        out_specs=pl.BlockSpec((SUBSTEPS, SUBLANES, width), lambda i: (0, i, 0)),
        compiler_params=params(),
        name="pick",
    )(place, own, speeds)


def advect_kernel(held, tall, step, own, far, own_edge, far_edge, speeds, masks, out, field):
    group = own.shape[0]
    total = group + 2 * SUBSTEPS
    lanes = field.shape[2]
    tiles = lanes // LANES
    for part in range(2):
        base = part * held

        def fill(spot, source, col, edge, edge_col):
            if held + tall != lanes:
                field[spot] = jnp.zeros((SUBLANES, lanes), F32)
            rows = edge[edge_col, :, part * tall : (part + 1) * tall]
            field[spot, :, :held] = source[col, :, base : base + held]
            field[spot, :, held : held + tall] = rows
            if held + tall != lanes:
                field[spot, :, lanes - tall :] = rows

        for col in range(group):
            fill(SUBSTEPS + col, own, col, own_edge, col)
        for col in range(SUBSTEPS):
            fill(col, far, col, far_edge, col)
            field[SUBSTEPS + group + col] = field[col]

        def spread(one):
            return jnp.concatenate([one] * tiles, axis=1)

        along, across = speeds[0, part, 0], speeds[0, part, 1]
        centre = spread(1.0 - jnp.abs(along) - jnp.abs(across))
        up = spread(jnp.maximum(along, 0.0)) * masks[total : total + 1, :]
        down = spread(-jnp.minimum(along, 0.0)) * masks[total + 1 : total + 2, :]
        side = spread(jnp.abs(across))
        forward = spread(across) > 0.0
        for turn in range(SUBSTEPS):
            first = turn + 1
            end = total - 1 - turn
            before = field[first - 1]
            here = field[first]
            for spot in range(first, end):
                after = field[spot + 1]
                upwind = jnp.where(forward, before, after)
                value = (
                    centre * here
                    + up * pltpu.roll(here, step, 1)
                    + down * pltpu.roll(here, lanes - step, 1)
                    + side * upwind
                ) * masks[spot : spot + 1, :]
                if turn == SUBSTEPS - 1:
                    out[spot - SUBSTEPS, :, base : base + held] = value[:, :held]
                else:
                    field[spot] = value
                before = here
                here = after


def advect(own, far, own_edge, far_edge, speeds, masks, first, tall, step, lanes):
    group, _, width = own.shape
    rows = far.shape[1]
    edge_lanes = own_edge.shape[2]
    total = group + 2 * SUBSTEPS
    return pl.pallas_call(
        functools.partial(advect_kernel, width // 2, tall, step),
        grid=(rows // SUBLANES,),
        out_shape=jax.ShapeDtypeStruct((group, rows, width), F32),
        in_specs=[
            pl.BlockSpec((group, SUBLANES, width), lambda i: (0, i, 0)),
            pl.BlockSpec((SUBSTEPS, SUBLANES, width), lambda i: (0, i, 0)),
            pl.BlockSpec((group, SUBLANES, edge_lanes), lambda i: (0, i, 0)),
            pl.BlockSpec((SUBSTEPS, SUBLANES, edge_lanes), lambda i: (0, i, 0)),
            pl.BlockSpec((1, 2, 2, SUBLANES, LANES), lambda i: (i + first, 0, 0, 0, 0)),
            pl.BlockSpec((total + 2, lanes), lambda i: (0, 0)),
        ],
        out_specs=pl.BlockSpec((group, SUBLANES, width), lambda i: (0, i, 0)),
        scratch_shapes=[pltpu.VMEM((total, SUBLANES, lanes), F32)],
        compiler_params=params(),
        name="advect",
    )(own, far, own_edge, far_edge, speeds, masks)


def unpack(source, turned, base, held):
    group, rows, _ = source.shape
    for row in range(0, rows, SUBLANES):
        for part in range(group):
            start = base + row * 2 * group + part * 2 * SUBLANES
            piece = source[part, row : row + SUBLANES, :]
            turned[start : start + SUBLANES, :] = piece[:, :held]
            turned[start + SUBLANES : start + 2 * SUBLANES, :] = piece[:, held:]


def profile(source, kernel_turned, offset, turned, held):
    unpack(source, turned, 0, held)
    high, low = halves(turned[...])
    kernel_high, kernel_low = halves(kernel_turned[:, offset : offset + turned.shape[0]])
    return (
        jnp.dot(kernel_high, high, preferred_element_type=F32)
        + jnp.dot(kernel_low, high, preferred_element_type=F32)
        + jnp.dot(kernel_high, low, preferred_element_type=F32)
    )


def partial_kernel(held, offset, source, kernel_turned, out, turned):
    out[...] = profile(source, kernel_turned, offset, turned, held)


def partial_profile(source, kernel_turned, offset):
    group, half, width = source.shape
    held = width // 2
    return pl.pallas_call(
        functools.partial(partial_kernel, held, offset),
        out_shape=jax.ShapeDtypeStruct((kernel_turned.shape[0], held), F32),
        in_specs=whole_vmem(2),
        out_specs=pl.BlockSpec(memory_space=VMEM),
        scratch_shapes=[pltpu.VMEM((group * 2 * half, held), F32)],
        compiler_params=params(),
        name="profile",
    )(source, kernel_turned)


def place_kernel(held, offset, depth, rows, per_row, pieces, *refs):
    source, kernel_turned = refs[:2]
    earlier = refs[2 : 2 + pieces]
    slots, column, out, turned, payload = refs[2 + pieces :]
    total = profile(source, kernel_turned, offset, turned, held)
    for piece in earlier:
        total = total + piece[...]
    payload[...] = jnp.zeros((2 * LANES, held), BF16)
    high, low = halves(total)
    payload[:depth, :] = high
    payload[LANES : LANES + depth, :] = low
    place = lax.broadcasted_iota(jnp.int32, (SUBLANES, held), 0)
    tag = jnp.where(place == 0, jnp.broadcast_to(column[...], (SUBLANES, held)) + 1, 0)
    tag_high, tag_low = halves(tag.astype(F32))
    payload[depth : depth + SUBLANES, :] = tag_high
    payload[LANES + depth : LANES + depth + SUBLANES, :] = tag_low
    out[...] = jnp.zeros(out.shape, F32)
    for turn in range(per_row):
        wanted = lax.broadcasted_iota(jnp.int32, (rows, held), 0) + turn * rows
        chosen = jnp.where(wanted == slots[...], 1.0, 0.0).astype(BF16)
        both = lax.dot_general(
            chosen, payload[...], (((1,), (1,)), ((), ())), preferred_element_type=F32
        )
        value = both[:, :LANES] + both[:, LANES:]
        out[:, turn * depth : (turn + 1) * depth] = value[:, :depth]
        spot = per_row * depth + turn
        out[:, spot : spot + 1] = value[:, depth : depth + 1]


def place_rows(source, kernel_turned, offset, earlier, slots, column, tiles, per_row, lanes):
    group, half, width = source.shape
    held = width // 2
    depth = kernel_turned.shape[0]
    rows = tiles * SUBLANES
    return pl.pallas_call(
        functools.partial(place_kernel, held, offset, depth, rows, per_row, len(earlier)),
        out_shape=jax.ShapeDtypeStruct((rows, lanes), F32),
        in_specs=whole_vmem(4 + len(earlier)),
        out_specs=pl.BlockSpec(memory_space=VMEM),
        scratch_shapes=[
            pltpu.VMEM((group * 2 * half, held), F32),
            pltpu.VMEM((2 * LANES, held), BF16),
        ],
        compiler_params=params(),
        name="place",
    )(source, kernel_turned, *earlier, slots, column)


def restore_kernel(held, comps, count, *refs):
    sources = refs[:count]
    out, turned = refs[count:]
    base = 0
    for source in sources:
        unpack(source, turned, base, held)
        base += source.shape[0] * source.shape[1] * 2
    for start in range(0, comps, LANES):
        size = min(LANES, comps - start)
        out[0, :, start : start + size] = turned[start : start + size, :].T


def restore(sources, comps):
    held = sources[0].shape[2] // 2
    padded = sum(s.shape[0] * s.shape[1] * 2 for s in sources)
    return pl.pallas_call(
        functools.partial(restore_kernel, held, comps, len(sources)),
        out_shape=jax.ShapeDtypeStruct((1, held, comps), F32),
        in_specs=whole_vmem(len(sources)),
        out_specs=pl.BlockSpec(memory_space=VMEM),
        scratch_shapes=[pltpu.VMEM((padded, held), F32)],
        compiler_params=params(),
        name="restore",
    )(*sources)


def slot_kernel(rows, owner_down, owner_across, out):
    held = owner_across.shape[1]
    down = lax.broadcasted_iota(jnp.int32, (held, held), 0)
    across = lax.broadcasted_iota(jnp.int32, (held, held), 1)
    same = (owner_down[...] == owner_across[...]) & (down < across)
    rank = jnp.sum(jnp.where(same, 1.0, 0.0), axis=0, keepdims=True).astype(jnp.int32)
    turn = rank >> 3
    out[...] = turn * rows + owner_across[...] * SUBLANES + (rank - turn * SUBLANES)


def slots_of(owner, tiles):
    held = owner.shape[0]
    return pl.pallas_call(
        functools.partial(slot_kernel, tiles * SUBLANES),
        out_shape=jax.ShapeDtypeStruct((1, held), jnp.int32),
        in_specs=whole_vmem(2),
        out_specs=pl.BlockSpec(memory_space=VMEM),
        compiler_params=params(),
        name="slot",
    )(owner, owner.reshape(1, held))


def flow_kernel(near, spin_ref, velocity, out):
    east, north = velocity[0, 0], velocity[0, 1]
    columns = east.shape[1]
    spot = lax.broadcasted_iota(jnp.int32, (columns, columns), 0)

    def chooser(index):
        return jnp.where(spot == near[index : index + 1, :], 1.0, 0.0)

    def thirds(value):
        high = value.astype(BF16)
        rest = value - high.astype(F32)
        middle = rest.astype(BF16)
        return high, middle, (rest - middle.astype(F32)).astype(BF16)

    def taken(value, plus, minus):
        difference = (chooser(plus) - chooser(minus)).astype(BF16)
        parts = [jnp.dot(part, difference, preferred_element_type=F32) for part in thirds(value)]
        return parts[0] + parts[1] + parts[2]

    zeta = taken(north, 0, 1) - taken(east, 2, 3)
    spin = spin_ref[...]
    out[0] = east + 0.25 * (spin * north)
    out[1] = north - 0.25 * (spin * east)
    out[2] = 0.25 * (spin + zeta)


def flow(near, spin, velocity):
    _, _, levels, columns = velocity.shape
    return pl.pallas_call(
        flow_kernel,
        out_shape=jax.ShapeDtypeStruct((3, levels, columns), F32),
        in_specs=whole_vmem(3),
        out_specs=pl.BlockSpec(memory_space=VMEM),
        compiler_params=params(),
        name="flow",
    )(near, spin, velocity)


def drift_kernel(depth, per_row, received, base, out):
    rows, _ = received.shape
    columns = base.shape[2]
    levels = depth // 2
    spot = lax.broadcasted_iota(jnp.int32, (rows, columns), 1).astype(F32) + 1.0
    total = jnp.zeros((2 * LANES, columns), F32)
    count = jnp.zeros((1, columns), F32)
    for turn in range(per_row):
        at = per_row * depth + turn
        hit = jnp.where(received[:, at : at + 1] == spot, 1.0, 0.0)
        count = count + jnp.sum(hit, axis=0, keepdims=True)
        piece = received[:, turn * depth : (turn + 1) * depth]
        piece = jnp.concatenate([piece, jnp.zeros((rows, LANES - depth), F32)], axis=1)
        high, low = halves(piece.T)
        total = total + jnp.dot(
            jnp.concatenate([high, low], axis=0), hit.astype(BF16), preferred_element_type=F32
        )
    drift = (total[:depth] + total[LANES : LANES + depth]) / jnp.maximum(count, 1.0)
    out[0, 0] = base[0] + base[2] * drift[levels:]
    out[0, 1] = base[1] - base[2] * drift[:levels]


def drifted(received, base, depth, per_row):
    _, levels, columns = base.shape
    return pl.pallas_call(
        functools.partial(drift_kernel, depth, per_row),
        out_shape=jax.ShapeDtypeStruct((1, 2, levels, columns), F32),
        in_specs=whole_vmem(2),
        out_specs=pl.BlockSpec(memory_space=VMEM),
        compiler_params=params(),
        name="drift",
    )(received, base)


def coupled_step(
    spectrum,
    interaction,
    comp_speed,
    sea_mask,
    stokes_kernel,
    tile_owner,
    ocean_column,
    neighbours,
    coriolis,
    velocity,
):
    local = spectrum[0]
    held, comps = local.shape
    width = lax.axis_size("pts")
    group = width // 2
    step = GC // width
    rows = held // step
    tall = SUBSTEPS * step
    lanes = round_up(held + tall, LANES)
    edge_lanes = round_up(2 * tall, LANES)
    unit = 2 * SUBLANES * group
    units = -(-comps // unit)
    padded = units * unit
    if padded > comps:
        extra = padded - comps
        local = jnp.pad(local, ((0, 0), (0, extra)))
        interaction = jnp.pad(interaction, ((0, extra), (0, extra)))
        comp_speed = jnp.pad(comp_speed, ((0, 0), (0, extra)))
        stokes_kernel = jnp.pad(stokes_kernel, ((0, extra), (0, 0)))
    kernel_turned = stokes_kernel.T
    depth = kernel_turned.shape[0]

    grid_index = lax.axis_index("grid")
    index = lax.axis_index("pts")
    side = index // group
    member = index % group
    place = jnp.stack([side, grid_index]).astype(jnp.int32)
    teams = [list(range(group)), list(range(group, width))]
    across = [(i, (i + group) % width) for i in range(width)]
    other_grid = [(0, 1), (1, 0)]

    open_sea = jnp.pad(
        sea_mask.astype(F32).reshape(2, rows, GC), ((0, 0), (0, 0), (SUBSTEPS, group + SUBSTEPS))
    )
    open_sea = lax.dynamic_slice_in_dim(open_sea, side * group, GC, 2)
    total = group + 2 * SUBSTEPS
    open_sea = open_sea.reshape(2, rows, step, width)[:, :, :, :total]
    open_sea = jnp.transpose(open_sea, (0, 3, 1, 2)).reshape(2, total, held)
    mine = jnp.where(grid_index == 0, open_sea[0], open_sea[1])
    edge_mask = jnp.where(grid_index == 0, open_sea[1][:, :tall], open_sea[0][:, held - tall :])
    if held + tall == lanes:
        masks = jnp.concatenate([mine, edge_mask], axis=1)
    else:
        gap = jnp.zeros((total, lanes - held - 2 * tall), F32)
        masks = jnp.concatenate([mine, edge_mask, gap, edge_mask], axis=1)
    lane = jnp.arange(lanes, dtype=jnp.int32)
    up_open = 1.0 - ((grid_index == 0) & (lane < step)).astype(F32)
    down_open = 1.0 - (
        (grid_index == 1) & (lane >= held - step) & (lane < held)
    ).astype(F32)
    masks = jnp.concatenate([masks, up_open[None], down_open[None]], axis=0)
    slots = slots_of(tile_owner[0], width)
    base = flow(neighbours[0].T, coriolis, velocity)

    speeds = comp_speed.reshape(2, units, group, 2, SUBLANES)
    speeds = lax.dynamic_index_in_dim(speeds, member, 2, keepdims=False)
    speeds = jnp.transpose(speeds, (1, 2, 0, 3))
    speeds = jnp.broadcast_to(speeds[..., None], speeds.shape + (LANES,))
    speeds, masks, kernel_turned = lax.optimization_barrier((speeds, masks, kernel_turned))

    team_exchange = functools.partial(
        lax.all_to_all,
        axis_name="pts",
        split_axis=0,
        concat_axis=0,
        tiled=True,
        axis_index_groups=teams,
    )
    plan = []
    first = 0
    for amount in split_units(units):
        plan.append((first, amount))
        first += amount
    count = len(plan)
    sent = []
    for first, amount in plan:
        sent.append(relax(local, interaction, group, first, amount))

    returned = []
    for number, (first, amount) in enumerate(plan):
        own = team_exchange(sent[number])
        send = pick(place, own, speeds, first, amount, step)
        if number + 1 < count:
            send, sent[number + 1] = lax.optimization_barrier((send, sent[number + 1]))
        far = lax.ppermute(send, "pts", across)
        edge = edges_of(place, own, tall, edge_lanes)
        own_edge = lax.ppermute(edge, "grid", other_grid)
        far_edge = edges_of(place, far, tall, edge_lanes)
        far_edge = lax.ppermute(far_edge, "grid", other_grid)
        moved = advect(own, far, own_edge, far_edge, speeds, masks, first, tall, step, lanes)
        returned.append(team_exchange(moved))

    capacity = 2 * held // width
    per_row = -(-capacity // SUBLANES)
    row_lanes = round_up(per_row * (depth + 1), LANES)

    earlier = [
        partial_profile(returned[n], kernel_turned, plan[n][0] * unit) for n in range(count - 1)
    ]
    buffer = place_rows(
        returned[-1],
        kernel_turned,
        plan[-1][0] * unit,
        earlier,
        slots,
        ocean_column,
        width,
        per_row,
        row_lanes,
    )
    received = lax.all_to_all(
        buffer.reshape(width, SUBLANES, row_lanes), "pts", split_axis=0, concat_axis=0, tiled=True
    )
    spectrum_next = restore(returned, comps)
    velocity_next = drifted(
        received.reshape(width * SUBLANES, row_lanes), base, depth, per_row
    )
    return (spectrum_next, velocity_next)


def solution(mesh):
    placed = (
        P("grid", "pts", None),
        P(),
        P(),
        P(),
        P(),
        P("grid", "pts", None),
        P("grid", "pts"),
        P("grid", "pts", None),
        P("grid", "pts"),
        P("grid", None, None, "pts"),
    )
    return jax.shard_map(
        coupled_step,
        mesh=mesh,
        in_specs=placed,
        out_specs=(P("grid", "pts", None), P("grid", None, None, "pts")),
        check_vma=False,
    )
```

time: 255 us -> 146 us (0.57)
  waiting for transfers between devices: 126 us -> 75.2 us
  local copies, waits for them, and re-layouts: 53.1 us -> 7.77 us
  Pallas kernels: 0 us -> 28.4 us
  other arithmetic: 24.8 us -> 0.2 us
  matrix products: 10.2 us -> 0 us
  starting transfers between devices: 39 us -> 33.3 us
    all_to_all x3 -> x5, waiting for transfers between devices: 126 us -> 30.9 us  [the longest x2 12.4 us: coupled_step(): returned.append(team_exchange(moved))]
    ppermute x4 -> x6, waiting for transfers between devices: 0.01 us -> 44.3 us  [the longest x2 41.8 us: coupled_step(): far = lax.ppermute(send, 'pts', across)]
    pallas_call x0 -> x16, Pallas kernels: none -> 28.4 us  [the longest x2 12.7 us: advect(): pl.pallas_call(functools.partial(advect_kernel, width // 2, tall, step),...]
    mul x5 -> x0, other arithmetic: 19.4 us -> none  [the longest x4 19.4 us: advect(): return result * mask]
    slice x13 -> x3, local copies, waits for them, and re-layouts: 16.8 us -> 0.39 us  [coupled_step(): mine = jnp.where(grid_index == 0, open_sea[0], open_sea[1])]
    all_to_all x3 -> x5, starting transfers between devices: 37.8 us -> 26.9 us  [the longest x2 13.4 us: coupled_step(): returned.append(team_exchange(moved))]
    dot_general x8 -> x0, matrix products: 10.2 us -> none  [the longest x1 5.13 us: per_device(): jnp.dot(local.astype(jnp.bfloat16), interaction, preferred_element_type=j...]
    another operation x13 -> x0, local copies, waits for them, and re-layouts: 9.78 us -> none  [the longest x12 6.13 us: per_device(): slabs = jnp.stack([field[:, :, :depth], field[:, :, held - depth:]], axis=1)]
  transfers between devices with their start and end apart: 7 -> 11, of which waited for: 3 -> 7; matrix products, arithmetic and copies ran while one was open for 8% -> 1% of each run, Pallas kernels for 0% -> 15%
where the time goes in v1:
time: 146 us
  waiting for transfers between devices  75.2 us (52%)
  starting transfers between devices  33.3 us (23%)
  Pallas kernels  28.4 us (19%)
  local copies, waits for them, and re-layouts  7.77 us (5%)
    ppermute x2, waiting for transfers between devices, coupled_step(): far = lax.ppermute(send, 'pts', across)  41.8 us
    all_to_all x2, starting transfers between devices, coupled_step(): returned.append(team_exchange(moved))  13.4 us
    pallas_call x2, Pallas kernels, advect(): pl.pallas_call(functools.partial(advect_kernel, width // 2, tall, step),...  12.7 us
    all_to_all x2, waiting for transfers between devices, coupled_step(): returned.append(team_exchange(moved))  12.4 us
    all_to_all x2, waiting for transfers between devices, coupled_step(): own = team_exchange(sent[number])  9.93 us
    all_to_all x2, starting transfers between devices, coupled_step(): own = team_exchange(sent[number])  9.91 us
    all_to_all x1, waiting for transfers between devices, coupled_step(): lax.all_to_all(buffer.reshape(width, SUBLANES, row_lanes), 'pts', split_a...  8.63 us
    unnamed x26, local copies, waits for them, and re-layouts  6.12 us
  transfers between devices with their start and end apart: 11, of which 7 were waited for; matrix products, arithmetic and copies ran while one was open for 1% of the time, Pallas kernels for 15%

profile of v1, /device:TPU:0, one launch (start us, length us, event | category | flops | bytes accessed | tf_op | source)
XLA Modules:
  0.0 145.8 jit_solution(17028656161840299387)
XLA Ops:
  0.6 0.0 copy-start
  0.6 1.7 %copy-done = bf16[1152,1152]{1,0:T(8,128)(2,1)S(1)} copy-done((bf16[1152,1152]{1,0:T(8,128)(2,1)S(1)}, bf16[1152,1152]{1,0:T(8,128)(2,1)}, u32[]{:S(2)}) %copy-start) | copy-done | bytes 2654232
  2.4 1.6 %copy-done.2 = f32[1,448,1152]{2,1,0:T(8,128)S(1)} copy-done((f32[1,448,1152]{2,1,0:T(8,128)S(1)}, f32[1,448,1152]{2,1,0:T(8,128)}, u32[]{:S(2)}) %copy-start.2) | copy-done | bytes 2064408
  4.0 1.5 %relax.2 = f32[8,40,896]{2,1,0:T(8,128)S(1)} custom-call(f32[448,1152]{1,0:T(8,128)S(1)} %bitcast.17, bf16[1152,1152]{1,0:T(8,128)(2,1)S(1)} %copy-done), custom_call_target="tpu_custom_call" | custom-call | tf_op jit(solution)/shard_map/relax/pallas_call | solution.py:80
  5.5 1.0 copy-done.4
  6.5 6.3 %all-to-all-start = ((f32[8,40,896]{2,1,0:T(8,128)}), f32[8,40,896]{2,1,0:T(8,128)S(1)}, u32[]{:S(2)}, u32[]{:S(2)}) async-start(f32[8,40,896]{2,1,0:T(8,128)} %copy-done.4), calls=%async_computation | async-start | bytes 2293760 | tf_op jit(solution)/shard_map/all_to_all | solution.py:547
  12.9 0.0 copy-start.1
  12.9 1.7 %copy-done.1 = bf16[1152,1152]{1,0:T(8,128)(2,1)S(1)} copy-done((bf16[1152,1152]{1,0:T(8,128)(2,1)S(1)}, bf16[1152,1152]{1,0:T(8,128)(2,1)}, u32[]{:S(2)}) %copy-start.1) | copy-done | bytes 2654232
  14.6 2.2 %relax.3 = f32[8,32,896]{2,1,0:T(8,128)} custom-call(f32[448,1152]{1,0:T(8,128)S(1)} %bitcast.18, bf16[1152,1152]{1,0:T(8,128)(2,1)S(1)} %copy-done.1), custom_call_target="tpu_custom_call" | custom-call | tf_op jit(solution)/shard_map/relax/pallas_call | solution.py:80
  16.9 0.0 copy-done.11
  16.9 0.1 reshape.67
  16.9 0.1 pad_dynamic-slice_fusion
  17.0 0.0 copy-start.12
  17.1 0.1 copy.19
  17.2 0.2 copy.20
  17.4 0.1 squeeze.23
  17.6 0.2 copy.21
  17.7 0.1 squeeze.24
  17.9 0.3 reshape.66
  18.2 0.1 copy.17
  18.3 0.1 copy.18
  18.4 0.1 pad_maximum_fusion.masks
  18.5 0.1 broadcast_in_dim.2.speeds
  18.6 0.1 pad_add_fusion.place
  18.7 9.9 %all-to-all-done.own.source = f32[8,40,896]{2,1,0:T(8,128)S(1)} async-done(((f32[8,40,896]{2,1,0:T(8,128)}), f32[8,40,896]{2,1,0:T(8,128)S(1)}, u32[]{:S(2)}, u32[]{:S(2)}) %all-to-all-start) | async-done | bytes 1146912 | tf_op jit(solution)/shard_map/all_to_all | solution.py:547
  28.6 1.3 pick.2
  29.9 3.6 %all-to-all-start.2 = ((f32[8,32,896]{2,1,0:T(8,128)}), f32[8,32,896]{2,1,0:T(8,128)S(1)}, u32[]{:S(2)}, u32[]{:S(2)}) async-start(f32[8,32,896]{2,1,0:T(8,128)} %relax.3), calls=%async_computation.2 | async-start | bytes 1835008 | tf_op jit(solution)/shard_map/all_to_all | solution.py:547
  33.5 2.7 %collective-permute-start = (f32[4,40,896]{2,1,0:T(8,128)S(1)}, f32[4,40,896]{2,1,0:T(8,128)S(1)}, u32[]{:S(2)}, u32[]{:S(2)}) collective-permute-start(f32[4,40,896]{2,1,0:T(8,128)S(1)} %pick.2), channel_id=1, source_target_pairs={{0,8},{1,9},{2,10},{3,11},{4,12},{5,13},{6,14},{7,15},{8,0},{9,1},... | collective-permute-start | bytes 1720328 | tf_op jit(solution)/shard_map/ppermute | solution.py:551
  36.2 0.6 edge.4
  36.8 0.1 collective-permute-start.1
  36.8 24.3 %collective-permute-done.source.far = f32[4,40,896]{2,1,0:T(8,128)S(1)} collective-permute-done((f32[4,40,896]{2,1,0:T(8,128)S(1)}, f32[4,40,896]{2,1,0:T(8,128)S(1)}, u32[]{:S(2)}, u32[]{:S(2)}) %collective-permute-start) | collective-permute-done | bytes 573472 | tf_op jit(solution)/shard_map/ppermute | solution.py:551
  61.1 0.6 edge.5
  61.7 0.1 collective-permute-start.2
  61.8 0.0 collective-permute-done.1.own_edge
  61.8 1.3 collective-permute-done.2.far_edge
  63.1 6.9 %advect.2 = f32[8,40,896]{2,1,0:T(8,128)} custom-call(f32[8,40,896]{2,1,0:T(8,128)S(1)} %all-to-all-done.own.source, f32[4,40,896]{2,1,0:T(8,128)S(1)} %collective-permute-done.source.far, f32[8,40,128]{2,1,0:T(8,128)S(1)} %collective-permute-done.1.own_edge, f32[4,40,128]{2,1,0:T(8,128)S(1)} %collective-permute-done.2.far_edge, ...), custom_call_target="tpu_custom_call" | custom-call | tf_op jit(solution)/shard_map/advect/pallas_call | solution.py:230
  70.0 0.0 all-to-all-done.2.own.source
  70.0 4.0 %all-to-all-start.1 = ((f32[8,40,896]{2,1,0:T(8,128)}), f32[8,40,896]{2,1,0:T(8,128)S(1)}, u32[]{:S(2)}, u32[]{:S(2)}) async-start(f32[8,40,896]{2,1,0:T(8,128)} %advect.2), calls=%async_computation.1 | async-start | bytes 2293760 | tf_op jit(solution)/shard_map/all_to_all | solution.py:557
  74.0 1.2 pick.3
  75.2 3.4 %collective-permute-start.3 = (f32[4,32,896]{2,1,0:T(8,128)S(1)}, f32[4,32,896]{2,1,0:T(8,128)S(1)}, u32[]{:S(2)}, u32[]{:S(2)}) collective-permute-start(f32[4,32,896]{2,1,0:T(8,128)S(1)} %pick.3), channel_id=1, source_target_pairs={{0,8},{1,9},{2,10},{3,11},{4,12},{5,13},{6,14},{7,15},{8,0},{9,1},... | collective-permute-start | bytes 1376264 | tf_op jit(solution)/shard_map/ppermute | solution.py:551
  78.6 0.6 edge.6
  79.2 0.1 collective-permute-start.4
  79.3 17.5 %collective-permute-done.3.source.far = f32[4,32,896]{2,1,0:T(8,128)S(1)} collective-permute-done((f32[4,32,896]{2,1,0:T(8,128)S(1)}, f32[4,32,896]{2,1,0:T(8,128)S(1)}, u32[]{:S(2)}, u32[]{:S(2)}) %collective-permute-start.3) | collective-permute-done | bytes 458784 | tf_op jit(solution)/shard_map/ppermute | solution.py:551
  96.8 0.6 edge.7
  97.3 0.1 collective-permute-start.5
  97.4 0.0 collective-permute-done.4.own_edge
  97.4 1.2 collective-permute-done.5.far_edge
  98.6 5.7 %advect.3 = f32[8,32,896]{2,1,0:T(8,128)} custom-call(f32[8,32,896]{2,1,0:T(8,128)S(1)} %all-to-all-done.2.own.source, f32[4,32,896]{2,1,0:T(8,128)S(1)} %collective-permute-done.3.source.far, f32[8,32,128]{2,1,0:T(8,128)S(1)} %collective-permute-done.4.own_edge, f32[4,32,128]{2,1,0:T(8,128)S(1)} %collective-permute-done.5.far_edge, ...), custom_call_target="tpu_custom_call" | custom-call | tf_op jit(solution)/shard_map/advect/pallas_call | solution.py:230
  104.4 0.0 all-to-all-done.1.refs_0_.source
  104.4 9.4 %all-to-all-start.3 = ((f32[8,32,896]{2,1,0:T(8,128)}), f32[8,32,896]{2,1,0:T(8,128)S(1)}, u32[]{:S(2)}, u32[]{:S(2)}) async-start(f32[8,32,896]{2,1,0:T(8,128)} %advect.3), calls=%async_computation.3 | async-start | bytes 1835008 | tf_op jit(solution)/shard_map/all_to_all | solution.py:557
  113.8 0.0 copy-done.7
  113.8 0.1 copy.22.owner_down
  113.9 0.2 slot.1.refs_3_
  114.1 0.7 profile.1.refs_2_
  114.8 0.0 copy-start.6
  114.8 0.0 copy-start.8
  114.8 0.0 copy-start.10
  114.8 12.4 %all-to-all-done.3.refs_1_.refs_0_ = f32[8,32,896]{2,1,0:T(8,128)S(1)} async-done(((f32[8,32,896]{2,1,0:T(8,128)}), f32[8,32,896]{2,1,0:T(8,128)S(1)}, u32[]{:S(2)}, u32[]{:S(2)}) %all-to-all-start.3) | async-done | bytes 917536 | tf_op jit(solution)/shard_map/all_to_all | solution.py:557
  127.2 2.2 %place.1 = f32[128,640]{1,0:T(8,128)} custom-call(f32[8,32,896]{2,1,0:T(8,128)S(1)} %all-to-all-done.3.refs_1_.refs_0_, f32[80,1152]{1,0:T(8,128)S(1)} %bitcast.20, f32[80,448]{1,0:T(8,128)S(1)} %profile.1.refs_2_, s32[1,448]{1,0:T(1,128)S(1)} %slot.1.refs_3_, s32[1,448]{1,0:T(1,128)S(1)} %copy-done.9), custom_call_target="tpu_custom_call" | custom-call | tf_op jit(solution)/shard_map/place/pallas_call | solution.py:322
  129.4 3.5 %all-to-all-start.4 = ((f32[16,8,640]{2,1,0:T(8,128)}), f32[16,8,640]{2,1,0:T(8,128)S(1)}, u32[]{:S(2)}, u32[]{:S(2)}) async-start(f32[16,8,640]{2,1,0:T(8,128)} %bitcast.11), calls=%async_computation.4 | async-start | bytes 655360 | tf_op jit(solution)/shard_map/all_to_all | solution.py:577
  133.0 0.3 flow.1.base
  133.3 2.3 %restore.1 = f32[1,448,1152]{2,1,0:T(8,128)} custom-call(f32[8,40,896]{2,1,0:T(8,128)S(1)} %all-to-all-done.1.refs_0_.source, f32[8,32,896]{2,1,0:T(8,128)S(1)} %all-to-all-done.3.refs_1_.refs_0_), custom_call_target="tpu_custom_call" | custom-call | tf_op jit(solution)/shard_map/restore/pallas_call | solution.py:351
  135.6 8.6 %all-to-all-done.4 = f32[16,8,640]{2,1,0:T(8,128)S(1)} async-done(((f32[16,8,640]{2,1,0:T(8,128)}), f32[16,8,640]{2,1,0:T(8,128)S(1)}, u32[]{:S(2)}, u32[]{:S(2)}) %all-to-all-start.4) | async-done | bytes 327712 | tf_op jit(solution)/shard_map/all_to_all | solution.py:577
  144.2 1.6 %drift.1 = f32[1,2,40,256]{3,2,1,0:T(8,128)} custom-call(f32[128,640]{1,0:T(8,128)S(1)} %bitcast.21, f32[3,40,256]{2,1,0:T(8,128)S(1)} %flow.1.base), custom_call_target="tpu_custom_call" | custom-call | tf_op jit(solution)/shard_map/drift/pallas_call | solution.py:446
  (20 shorter events, 0.1 us)
Async XLA Ops:
  0.6 1.8 %copy-start = (bf16[1152,1152]{1,0:T(8,128)(2,1)S(1)}, bf16[1152,1152]{1,0:T(8,128)(2,1)}, u32[]{:S(2)}) copy-start(bf16[1152,1152]{1,0:T(8,128)(2,1)} %weights.3) | copy-start | bytes 7962628
  2.4 1.6 %copy-start.2 = (f32[1,448,1152]{2,1,0:T(8,128)S(1)}, f32[1,448,1152]{2,1,0:T(8,128)}, u32[]{:S(2)}) copy-start(f32[1,448,1152]{2,1,0:T(8,128)} %param.10) | copy-start | bytes 6193156
  5.5 1.0 copy-start.4
  6.5 6.3 %copy-start.3 = (f32[1,448,1152]{2,1,0:T(8,128)S(1)}, f32[1,448,1152]{2,1,0:T(8,128)}, u32[]{:S(2)}) copy-start(f32[1,448,1152]{2,1,0:T(8,128)} %param.10) | copy-start | bytes 6193156
  6.5 22.1 %all-to-all-start = ((f32[8,40,896]{2,1,0:T(8,128)}), f32[8,40,896]{2,1,0:T(8,128)S(1)}, u32[]{:S(2)}, u32[]{:S(2)}) async-start(f32[8,40,896]{2,1,0:T(8,128)} %copy-done.4), calls=%async_computation | async-start | bytes 2293760 | tf_op jit(solution)/shard_map/all_to_all | solution.py:547
  12.9 1.8 %copy-start.1 = (bf16[1152,1152]{1,0:T(8,128)(2,1)S(1)}, bf16[1152,1152]{1,0:T(8,128)(2,1)}, u32[]{:S(2)}) copy-start(bf16[1152,1152]{1,0:T(8,128)(2,1)} %weights.3) | copy-start | bytes 7962628
  14.6 2.2 %copy-start.11 = (s32[2,7168]{1,0:T(2,128)S(1)}, s32[2,7168]{1,0:T(2,128)}, u32[]{:S(2)}) copy-start(s32[2,7168]{1,0:T(2,128)} %param.13) | copy-start | bytes 172036
  17.0 0.8 copy-start.12
  29.9 40.0 %all-to-all-start.2 = ((f32[8,32,896]{2,1,0:T(8,128)}), f32[8,32,896]{2,1,0:T(8,128)S(1)}, u32[]{:S(2)}, u32[]{:S(2)}) async-start(f32[8,32,896]{2,1,0:T(8,128)} %relax.3), calls=%async_computation.2 | async-start | bytes 1835008 | tf_op jit(solution)/shard_map/all_to_all | solution.py:547
  33.5 27.6 %collective-permute-start = (f32[4,40,896]{2,1,0:T(8,128)S(1)}, f32[4,40,896]{2,1,0:T(8,128)S(1)}, u32[]{:S(2)}, u32[]{:S(2)}) collective-permute-start(f32[4,40,896]{2,1,0:T(8,128)S(1)} %pick.2), channel_id=1, source_target_pairs={{0,8},{1,9},{2,10},{3,11},{4,12},{5,13},{6,14},{7,15},{8,0},{9,1},... | collective-permute-start | bytes 1720328 | tf_op jit(solution)/shard_map/ppermute | solution.py:551
  36.8 25.0 %collective-permute-start.1 = (f32[8,40,128]{2,1,0:T(8,128)S(1)}, f32[8,40,128]{2,1,0:T(8,128)S(1)}, u32[]{:S(2)}, u32[]{:S(2)}) collective-permute-start(f32[8,40,128]{2,1,0:T(8,128)S(1)} %edge.4), channel_id=1, source_target_pairs={{0,16},{16,0},{1,17},{17,1},{2,18},{18,2},{3,19},{19,3},{4,20},{20... | collective-permute-start | bytes 491528 | tf_op jit(solution)/shard_map/ppermute | solution.py:553
  61.7 1.3 collective-permute-start.2
  70.0 34.4 %all-to-all-start.1 = ((f32[8,40,896]{2,1,0:T(8,128)}), f32[8,40,896]{2,1,0:T(8,128)S(1)}, u32[]{:S(2)}, u32[]{:S(2)}) async-start(f32[8,40,896]{2,1,0:T(8,128)} %advect.2), calls=%async_computation.1 | async-start | bytes 2293760 | tf_op jit(solution)/shard_map/all_to_all | solution.py:557
  75.2 21.6 %collective-permute-start.3 = (f32[4,32,896]{2,1,0:T(8,128)S(1)}, f32[4,32,896]{2,1,0:T(8,128)S(1)}, u32[]{:S(2)}, u32[]{:S(2)}) collective-permute-start(f32[4,32,896]{2,1,0:T(8,128)S(1)} %pick.3), channel_id=1, source_target_pairs={{0,8},{1,9},{2,10},{3,11},{4,12},{5,13},{6,14},{7,15},{8,0},{9,1},... | collective-permute-start | bytes 1376264 | tf_op jit(solution)/shard_map/ppermute | solution.py:551
  79.2 18.2 %collective-permute-start.4 = (f32[8,32,128]{2,1,0:T(8,128)S(1)}, f32[8,32,128]{2,1,0:T(8,128)S(1)}, u32[]{:S(2)}, u32[]{:S(2)}) collective-permute-start(f32[8,32,128]{2,1,0:T(8,128)S(1)} %edge.6), channel_id=1, source_target_pairs={{0,16},{16,0},{1,17},{17,1},{2,18},{18,2},{3,19},{19,3},{4,20},{20... | collective-permute-start | bytes 393224 | tf_op jit(solution)/shard_map/ppermute | solution.py:553
  97.3 1.3 collective-permute-start.5
  104.4 9.4 %copy-start.7 = (s32[1,448,1]{1,2,0:T(1,128)S(1)}, s32[1,448,1]{1,2,0:T(1,128)}, u32[]{:S(2)}) copy-start(s32[1,448,1]{1,2,0:T(1,128)} %param.15) | copy-start | bytes 5380
  104.4 9.7 %copy-start.5 = (f32[1152,80]{0,1:T(8,128)S(1)}, f32[1152,80]{0,1:T(8,128)}, u32[]{:S(2)}) copy-start(f32[1152,80]{0,1:T(8,128)} %param.14) | copy-start | bytes 1105924
  104.4 22.8 %all-to-all-start.3 = ((f32[8,32,896]{2,1,0:T(8,128)}), f32[8,32,896]{2,1,0:T(8,128)S(1)}, u32[]{:S(2)}, u32[]{:S(2)}) async-start(f32[8,32,896]{2,1,0:T(8,128)} %advect.3), calls=%async_computation.3 | async-start | bytes 1835008 | tf_op jit(solution)/shard_map/all_to_all | solution.py:557
  113.8 13.5 %copy-start.9 = (s32[1,448]{1,0:T(1,128)S(1)}, s32[1,448]{1,0:T(1,128)}, u32[]{:S(2)}) copy-start(s32[1,448]{1,0:T(1,128)} %refs_4_.1) | copy-start | bytes 5380
  114.8 18.1 %copy-start.6 = (f32[1,2,40,256]{3,2,1,0:T(8,128)S(1)}, f32[1,2,40,256]{3,2,1,0:T(8,128)}, u32[]{:S(2)}) copy-start(f32[1,2,40,256]{3,2,1,0:T(8,128)} %velocity.1) | copy-start | bytes 245764
  114.8 18.1 %copy-start.8 = (s32[1,256,4]{1,2,0:T(4,128)S(1)}, s32[1,256,4]{1,2,0:T(4,128)}, u32[]{:S(2)}) copy-start(s32[1,256,4]{1,2,0:T(4,128)} %param.17) | copy-start | bytes 12292
  114.8 18.1 %copy-start.10 = (f32[1,256]{1,0:T(1,128)S(1)}, f32[1,256]{1,0:T(1,128)}, u32[]{:S(2)}) copy-start(f32[1,256]{1,0:T(1,128)} %spin_ref.1) | copy-start | bytes 3076
  129.4 14.8 %all-to-all-start.4 = ((f32[16,8,640]{2,1,0:T(8,128)}), f32[16,8,640]{2,1,0:T(8,128)S(1)}, u32[]{:S(2)}, u32[]{:S(2)}) async-start(f32[16,8,640]{2,1,0:T(8,128)} %bitcast.11), calls=%async_computation.4 | async-start | bytes 655360 | tf_op jit(solution)/shard_map/all_to_all | solution.py:577
